TPU v7x, 32 devices: a whole 2x2x4 slice. The times are simulated.
32 devices in a mesh: grp: 2 (over y), smp: 8 (over z, x), feat: 2 (over core).
Axes of the slice: x: 2, y: 2, z: 4, core: 2. Of those that a mesh axis runs over, the one named last changes fastest.
Arguments:
- coal_size: int32 [1024], P(('grp', 'smp')), parts along dimension 0, may hold values from 1536 to 2559
- coal_step: int32 [1024], P(('grp', 'smp')), parts along dimension 0, may hold values from 0 to 2047
- coal_shift: int32 [1024], P(('grp', 'smp')), parts along dimension 0, may hold values from 0 to 4095
- outputs_y: float32 [1024, 32], P(('grp', 'smp')), parts along dimension 0, may hold values from -6 to 6
Outputs:
- attributions: float32 [8192, 32], P(('grp', 'smp', 'feat')), parts along dimension 0
- residual: float32 [8192, 32], P(('grp', 'smp', 'feat')), parts along dimension 0
There are 2 independent parts, one for each index of `grp`. A program takes and returns all parts, laid end to end along the dimension named above; each array names one. Nothing has to cross between parts.
All inputs are finite; a program needn't handle non-finite values.
Results may differ from a plain program's by a relative error of at most 0.0003.
Values sent between devices are 32-bit elements; how exact they have to be, the bound alone decides.
A program may use at most 64 MiB of HBM per device.

v0:
```python
import jax
import jax.numpy as jnp
from jax import lax
from jax.sharding import PartitionSpec as P

F = 4096
ITERS = 2


RIDGE = 1.0
HIGH = lax.Precision.HIGHEST


def contract_rows(left, right):
    return lax.dot_general(
        left, right, (((0,), (0,)), ((), ())), precision=HIGH, preferred_element_type=jnp.float32
    )


def body(coal_size, coal_step, coal_shift, outputs_y):
    n_smp = lax.axis_size("smp")
    n_feat = lax.axis_size("feat")
    half = F // n_feat
    share = half // n_smp
    samples = coal_size.shape[0] * n_smp
    feat_index = lax.axis_index("feat")
    local = jnp.arange(half, dtype=jnp.int32)
    columns = (local // share * n_feat + feat_index) * share + local % share
    mult = 2 * coal_step + 1
    coded = (columns[None, :] * mult[:, None] + coal_shift[:, None]) % F
    masks = 2.0 * (coded < coal_size[:, None]).astype(jnp.float32) - 1.0
    kf = coal_size.astype(jnp.float32)
    weights = F * (F - 1) / (kf * (F - kf) * samples)
    first = weights[:, None] * outputs_y

    def totals(scaled):
        return lax.psum(contract_rows(masks, scaled), "smp")

    def column_dots(product):
        return lax.psum(jnp.sum(product, axis=0), "feat")

    target = totals(first)
    attributions = jnp.zeros_like(target)
    residual = target
    direction = target
    norm_now = column_dots(residual * residual)
    for step in range(ITERS):
        part = jnp.dot(masks, direction, precision=HIGH, preferred_element_type=jnp.float32)
        image = totals(weights[:, None] * lax.psum(part, "feat")) + RIDGE * direction
        alpha = norm_now / column_dots(direction * image)
        attributions = attributions + alpha * direction
        residual = residual - alpha * image
        norm_next = column_dots(residual * residual)
        direction = residual + norm_next / norm_now * direction
        norm_now = norm_next
    offset = lax.axis_index("smp") * share
    attributions = lax.dynamic_slice_in_dim(attributions, offset, share, 0)
    residual = lax.dynamic_slice_in_dim(residual, offset, share, 0)
    return (attributions, residual)


def solution(mesh):
    placed = (P(("grp", "smp")), P(("grp", "smp")), P(("grp", "smp")), P(("grp", "smp"), None))
    return jax.shard_map(
        body,
        mesh=mesh,
        in_specs=placed,
        out_specs=(P(("grp", "smp", "feat"), None), P(("grp", "smp", "feat"), None)),
        check_vma=False,
    )
```

profile of v0, /device:TPU:0, one launch (start us, length us, event | category | flops | bytes accessed | tf_op | source)
XLA Modules:
  0.0 255.6 jit_solution(13662654553047194472)
XLA Ops:
  7.2 0.0 copy-start.1
  7.2 0.0 all-reduce.5.cloned.1.call-start
  7.2 0.7 multiply_add_fusion.1
  7.9 0.7 fusion.41
  8.5 0.0 copy-start.2
  8.5 0.0 copy-start.3
  8.6 0.0 copy-done.1
  8.6 0.6 copy-done.2
  9.2 0.0 copy-done.3
  9.2 1.5 fusion.6
  10.7 0.0 all-reduce.5.cloned.1.call-update
  10.7 0.0 all-reduce.7.cloned.1.call-start
  10.8 74.3 %all-reduce.5.cloned.1.call-done = f32[2048,32]{0,1:T(8,128)} async-done(((f32[2048,32]{0,1:T(8,128)}), f32[2048,32]{0,1:T(8,128)}) %all-reduce.5.cloned.1.call-update) | async-done | bytes 262160 | tf_op jit(solution)/shard_map/psum | solution.py:37
  85.1 1.8 fusion.5
  86.9 3.4 %psum.65 = f32[64,32]{0,1:T(8,128)S(1)} all-reduce(f32[64,32]{0,1:T(8,128)S(1)} %fusion.5), channel_id=1, replica_groups=mesh['grp'=2,'smp'=8,'feat'=2] {'feat'}, use_global_device_ids=true, to_apply=%region_3.4 | all-reduce | flops 2048 | bytes 16384 | tf_op jit(solution)/shard_map/psum | solution.py:49
  90.3 1.5 fusion.4
  91.8 0.0 copy-start
  91.8 0.0 all-reduce.7.cloned.1.call-update
  91.8 0.0 all-reduce.9.cloned.1.call-start
  91.8 70.4 %all-reduce.7.cloned.1.call-done = f32[2048,32]{0,1:T(8,128)} async-done(((f32[2048,32]{0,1:T(8,128)}), f32[2048,32]{0,1:T(8,128)}) %all-reduce.7.cloned.1.call-update) | async-done | bytes 262160 | tf_op jit(solution)/shard_map/psum | solution.py:37
  162.2 0.0 copy-done
  162.2 1.1 multiply_reduce_fusion.2
  163.3 2.5 all-reduce
  165.8 0.2 multiply_reduce_fusion.1
  166.0 2.5 psum.68
  168.5 0.1 multiply_add_fusion
  168.6 0.9 fusion.3
  169.5 3.4 %psum.69 = f32[64,32]{0,1:T(8,128)S(1)} all-reduce(f32[64,32]{0,1:T(8,128)S(1)} %fusion.3), channel_id=1, replica_groups=mesh['grp'=2,'smp'=8,'feat'=2] {'feat'}, use_global_device_ids=true, to_apply=%region_9.10 | all-reduce | flops 2048 | bytes 16384 | tf_op jit(solution)/shard_map/psum | solution.py:49
  172.8 1.5 fusion.2
  174.3 0.0 all-reduce.9.cloned.1.call-update
  174.3 70.4 %all-reduce.9.cloned.1.call-done = f32[2048,32]{0,1:T(8,128)} async-done(((f32[2048,32]{0,1:T(8,128)}), f32[2048,32]{0,1:T(8,128)}) %all-reduce.9.cloned.1.call-update) | async-done | bytes 262160 | tf_op jit(solution)/shard_map/psum | solution.py:37
  244.8 1.1 multiply_reduce_fusion
  245.8 2.5 psum.71
  248.3 0.7 dynamic-slice_subtract_fusion
  (4 shorter events, 0.0 us)
Async XLA Ops:
  7.2 1.4 copy-start.1
  7.2 77.9 %all-reduce.5.cloned.1.call-start = ((), (), s32[]{:S(2)}) async-start(), calls=%async_computation | async-start | bytes 524288 | tf_op jit(solution)/shard_map/psum | solution.py:37
  8.5 0.7 copy-start.2
  8.5 0.7 copy-start.3
  10.7 151.5 %all-reduce.7.cloned.1.call-start = ((), (), s32[]{:S(2)}) async-start(), calls=%async_computation.1 | async-start | bytes 524288 | tf_op jit(solution)/shard_map/psum | solution.py:37
  91.8 70.5 %copy-start = (f32[2048,32]{0,1:T(8,128)S(1)}, f32[2048,32]{0,1:T(8,128)}, u32[]{:S(2)}) copy-start(f32[2048,32]{0,1:T(8,128)} %all-reduce.5.cloned.1.call-done) | copy-start | bytes 786436
  91.8 153.0 %all-reduce.9.cloned.1.call-start = ((), (), s32[]{:S(2)}) async-start(), calls=%async_computation.2 | async-start | bytes 524288 | tf_op jit(solution)/shard_map/psum | solution.py:37
Sparse Core Ops, SparseCore 0:
  11.3 73.7 all-reduce.4
  91.9 70.2 all-reduce.6
  174.4 70.2 all-reduce.8
where the time goes:
time: 256 us
  waiting for transfers between devices  215 us (84%)
  blocking collectives  14.1 us (6%)
  between operations  13.8 us (5%)
  matrix products  7.05 us (3%)
  other arithmetic  4.57 us (2%)
    psum x3, waiting for transfers between devices, totals(): return lax.psum(contract_rows(masks, scaled), 'smp')  215 us
    psum x3, blocking collectives, column_dots(): return lax.psum(jnp.sum(product, axis=0), 'feat')  7.4 us
    psum x2, blocking collectives, body(): lax.psum(part, 'feat')  6.73 us
  transfers between devices with their start and end apart: 3, of which 3 were waited for; matrix products, arithmetic and copies ran while one was open for 0% of the time, Pallas kernels for 0%

commit v1 on v0

--- a/solution.py
+++ b/solution.py
@@ -1,14 +1,21 @@
+import functools
+
 import jax
 import jax.numpy as jnp
 from jax import lax
+from jax.experimental import pallas as pl
+from jax.experimental.pallas import tpu as pltpu
 from jax.sharding import PartitionSpec as P
 
 F = 4096
+R = 32
 ITERS = 2
-
 
 RIDGE = 1.0
 HIGH = lax.Precision.HIGHEST
+LANES = 128
+GRAM_LIMIT = 512
+LOW = -(2 ** 31)
 
 
 def contract_rows(left, right):
@@ -59,10 +66,160 @@
     return (attributions, residual)
 
 
+def split(v):
+    a = v.astype(jnp.bfloat16)
+    v = v - a.astype(jnp.float32)
+    b = v.astype(jnp.bfloat16)
+    v = v - b.astype(jnp.float32)
+    return jnp.concatenate([a, b, v.astype(jnp.bfloat16)], axis=0)
+
+
+def join(v, rows):
+    return v[:rows] + (v[rows:2 * rows] + v[2 * rows:])
+
+
+def mm(a, b):
+    return jnp.dot(a, b, preferred_element_type=jnp.float32)
+
+
+def kernel(n, n_feat, size_ref, step_ref, shift_ref, y_ref, out_ref,
+           coal, ys, masks, send_c, recv_c, send_y, recv_y):
+    me = lax.axis_index("smp")
+    own = size_ref.shape[1]
+    samples = own * n
+    share = F // (n * n_feat)
+
+    coal[me, 0:1, 0:own] = size_ref[...].astype(jnp.float32)
+    coal[me, 1:2, 0:own] = step_ref[...].astype(jnp.float32)
+    coal[me, 2:3, 0:own] = shift_ref[...].astype(jnp.float32)
+    yt = y_ref[...].T
+    ys[me, :, 0:own] = yt[: R // 2]
+    ys[me, :, own:2 * own] = yt[R // 2:]
+
+    barrier = pltpu.get_barrier_semaphore()
+    for k in range(1, n):
+        pl.semaphore_signal(barrier, inc=1, device_id={"smp": lax.rem(me + k, n)})
+    pl.semaphore_wait(barrier, n - 1)
+
+    coal_copies, y_copies = [], []
+    for k in range(1, n):
+        copy = pltpu.make_async_remote_copy(
+            src_ref=coal.at[me], dst_ref=coal.at[me], send_sem=send_c.at[k], recv_sem=recv_c.at[k],
+            device_id={"smp": lax.rem(me + k, n)})
+        copy.start()
+        coal_copies.append(copy)
+    for k in range(1, n):
+        copy = pltpu.make_async_remote_copy(
+            src_ref=ys.at[me], dst_ref=ys.at[me], send_sem=send_y.at[k], recv_sem=recv_y.at[k],
+            device_id={"smp": lax.rem(me + k, n)})
+        copy.start()
+        y_copies.append(copy)
+
+    lane = lax.broadcasted_iota(jnp.int32, (own, LANES), 1)
+    one = jnp.full((own, LANES), 1.0, jnp.float32)
+    for k in range(n):
+        peer = lax.rem(me + n - k, n)
+        if k:
+            coal_copies[k - 1].wait_recv()
+        cols = coal[peer].T[0:own].astype(jnp.int32)
+        size = jnp.broadcast_to(cols[:, 0:1], (own, LANES))
+        mult = 2 * jnp.broadcast_to(cols[:, 1:2], (own, LANES)) + 1
+        shift = jnp.broadcast_to(cols[:, 2:3], (own, LANES))
+        code = ((lane * mult + shift) << 20) + LOW
+        limit = (size << 20) + LOW
+        stride = mult << 27
+        rows = pl.ds(pl.multiple_of(peer * own, own), own)
+        for c in range(F // LANES):
+            masks[rows, c * LANES:(c + 1) * LANES] = jnp.where(code < limit, one, -one).astype(masks.dtype)
+            code = code + stride
+
+    m = masks[...]
+    gram = lax.dot_general(m, m, (((1,), (1,)), ((), ())), preferred_element_type=jnp.float32)
+    gram_hi = gram.astype(jnp.bfloat16)
+    gram_lo = (gram - gram_hi.astype(jnp.float32)).astype(jnp.bfloat16)
+
+    def by_gram(v):
+        s = split(v)
+        return join(mm(s, gram_hi) + mm(s, gram_lo), R)
+
+    left = lax.broadcasted_iota(jnp.int32, (R // 2, LANES), 1) < own
+    kf, y = [], []
+    for copy in y_copies:
+        copy.wait_recv()
+    for q in range(0, n, 2):
+        t0, t1 = coal[q, 0:1], coal[q + 1, 0:1]
+        kf.append(jnp.where(left[0:1], t0, pltpu.roll(t1, own, 1)))
+        t0, t1 = ys[q], ys[q + 1]
+        y.append(jnp.concatenate([
+            jnp.where(left, t0, pltpu.roll(t1, own, 1)),
+            jnp.where(left, pltpu.roll(t0, own, 1), t1)], axis=0))
+    kf = jnp.concatenate(kf, axis=1)
+    y = jnp.concatenate(y, axis=1)
+    weights = F * (F - 1) / (kf * (F - kf) * samples)
+
+    def dots(product):
+        return jnp.sum(product, axis=1, keepdims=True)
+
+    residual = weights * y
+    direction = residual
+    seen = by_gram(residual)
+    norm_now = dots(residual * seen)
+    attributions = jnp.zeros_like(residual)
+    for step in range(ITERS):
+        image = weights * seen + RIDGE * direction
+        alpha = norm_now / dots(seen * image)
+        attributions = attributions + alpha * direction
+        residual = residual - alpha * image
+        if step < ITERS - 1:
+            fresh = by_gram(residual)
+            norm_next = dots(residual * fresh)
+            beta = norm_next / norm_now
+            direction = residual + beta * direction
+            seen = fresh + beta * seen
+            norm_now = norm_next
+
+    place = me * n_feat + lax.axis_index("feat")
+    mine = masks[:, pl.ds(pl.multiple_of(place * share, share), share)]
+    both = jnp.concatenate([attributions, residual], axis=0)
+    out_ref[...] = join(mm(split(both), mine), 2 * R)
+    for copy in coal_copies + y_copies:
+        copy.wait_send()
+
+
+def gram_body(n, n_feat, coal_size, coal_step, coal_shift, outputs_y):
+    own = coal_size.shape[0]
+    share = F // (n * n_feat)
+    out = pl.pallas_call(
+        functools.partial(kernel, n, n_feat),
+        out_shape=jax.ShapeDtypeStruct((2 * R, share), jnp.float32),
+        in_specs=[pl.BlockSpec(memory_space=pltpu.VMEM)] * 4,
+        out_specs=pl.BlockSpec(memory_space=pltpu.VMEM),
+        scratch_shapes=[
+            pltpu.VMEM((n, 8, LANES), jnp.float32),
+            pltpu.VMEM((n, R // 2, LANES), jnp.float32),
+            pltpu.VMEM((own * n, F), jnp.bfloat16),
+            pltpu.SemaphoreType.DMA((n,)),
+            pltpu.SemaphoreType.DMA((n,)),
+            pltpu.SemaphoreType.DMA((n,)),
+            pltpu.SemaphoreType.DMA((n,)),
+        ],
+        compiler_params=pltpu.CompilerParams(collective_id=0, has_side_effects=True),
+    )(coal_size.reshape(1, own), coal_step.reshape(1, own), coal_shift.reshape(1, own), outputs_y)
+    return out[:R].T, out[R:].T
+
+
 def solution(mesh):
+    n, n_feat = mesh.shape["smp"], mesh.shape["feat"]
+
+    def chosen(coal_size, coal_step, coal_shift, outputs_y):
+        own = coal_size.shape[0]
+        if own * n <= GRAM_LIMIT and 2 * own == LANES and n % 2 == 0:
+            return gram_body(n, n_feat, coal_size, coal_step, coal_shift, outputs_y)
+        return body(coal_size, coal_step, coal_shift, outputs_y)
+
     placed = (P(("grp", "smp")), P(("grp", "smp")), P(("grp", "smp")), P(("grp", "smp"), None))
     return jax.shard_map(
-        body,
+        chosen,
         mesh=mesh,
         in_specs=placed,
         out_specs=(P(("grp", "smp", "feat"), None), P(("grp", "smp", "feat"), None)),

time: 256 us -> 19.3 us (0.08)
  waiting for transfers between devices: 215 us -> 0 us
  Pallas kernels: 0 us -> 15.6 us
  blocking collectives: 14.1 us -> 0 us
  between operations: 13.8 us -> 0.64 us
  matrix products: 7.05 us -> 0 us
  other arithmetic: 4.57 us -> 0 us
    psum x3 -> x0, waiting for transfers between devices: 215 us -> none  [totals(): return lax.psum(contract_rows(masks, scaled), 'smp')]
    pallas_call x0 -> x1, Pallas kernels: none -> 15.6 us  [gram_body(): pl.pallas_call(functools.partial(kernel, n, n_feat), out_shape=jax.ShapeD...]
    psum x5 -> x0, blocking collectives: 14.1 us -> none  [the longest x3 7.4 us: column_dots(): return lax.psum(jnp.sum(product, axis=0), 'feat')]
    dot_general x5 -> x0, matrix products: 7.05 us -> none  [the longest x3 4.4 us: contract_rows(): lax.dot_general(left, right, (((0,), (0,)), ((), ())), precision=HIGH, pr...]
  transfers between devices with their start and end apart: 3 -> 0, of which waited for: 3 -> 0; matrix products, arithmetic and copies ran while one was open for 0% -> 0% of each run, Pallas kernels for 0% -> 0%
where the time goes in v1:
time: 19.3 us; the launch traced here: 19 us
  Pallas kernels  15.6 us (81%)
  local copies, waits for them, and re-layouts  2.82 us (15%)
  between operations  0.64 us (3%)
    pallas_call x1, Pallas kernels, gram_body(): pl.pallas_call(functools.partial(kernel, n, n_feat), out_shape=jax.ShapeD...  15.6 us
    unnamed x1, local copies, waits for them, and re-layouts  1.41 us
    transpose x1, local copies, waits for them, and re-layouts, gram_body(): return (out[:R].T, out[R:].T)  1.4 us

profile of v1, /device:TPU:0, one launch (start us, length us, event | category | flops | bytes accessed | tf_op | source)
XLA Modules:
  0.0 19.0 jit_solution(17779939067678548730)
XLA Ops:
  0.6 1.4 %copy.6.y_ref = f32[64,32]{1,0:T(8,128)} copy(f32[64,32]{0,1:T(8,128)} %param.7) | data formatting | bytes 16384 | tf_op args[3]
  2.0 15.6 %shard_map.59 = f32[64,256]{1,0:T(8,128)} custom-call(s32[1,64]{1,0:T(1,128)} %bitcast.7, s32[1,64]{1,0:T(1,128)} %bitcast.8, s32[1,64]{1,0:T(1,128)} %bitcast.9, f32[64,32]{1,0:T(8,128)} %copy.6.y_ref), custom_call_target="tpu_custom_call" | custom-call | tf_op jit(solution)/shard_map/pallas_call | solution.py:192
  17.6 1.4 %slice_bitcast_fusion = (f32[256,32]{0,1:T(8,128)}, f32[256,32]{0,1:T(8,128)}) fusion(f32[64,256]{1,0:T(8,128)} %shard_map.59), kind=kLoop, calls=%fused_computation | loop fusion | bytes 131072 | tf_op jit(solution)/shard_map/transpose | solution.py:208

commit v2 on v1

--- a/solution.py
+++ b/solution.py
@@ -16,6 +16,9 @@
 LANES = 128
 GRAM_LIMIT = 512
 LOW = -(2 ** 31)
+CODES = 4
+MASK_TYPE = jnp.float8_e4m3fn
+VMEM_BYTES = 20 * 2 ** 20
 
 
 def contract_rows(left, right):
@@ -78,74 +81,99 @@
     return v[:rows] + (v[rows:2 * rows] + v[2 * rows:])
 
 
+def mm_nt(a, b):
+    return lax.dot_general(a, b, (((1,), (1,)), ((), ())), preferred_element_type=jnp.float32)
+
+
 def mm(a, b):
     return jnp.dot(a, b, preferred_element_type=jnp.float32)
 
 
-def kernel(n, n_feat, size_ref, step_ref, shift_ref, y_ref, out_ref,
-           coal, ys, masks, send_c, recv_c, send_y, recv_y):
+def kernel(n, n_feat, size_in, step_in, shift_in, y_in, out_ref,
+           ints, y_own, coal, ys, masks, in_sem, send_c, recv_c, send_y, recv_y):
     me = lax.axis_index("smp")
-    own = size_ref.shape[1]
+    own = size_in.shape[1]
     samples = own * n
     share = F // (n * n_feat)
-
-    coal[me, 0:1, 0:own] = size_ref[...].astype(jnp.float32)
-    coal[me, 1:2, 0:own] = step_ref[...].astype(jnp.float32)
-    coal[me, 2:3, 0:own] = shift_ref[...].astype(jnp.float32)
-    yt = y_ref[...].T
-    ys[me, :, 0:own] = yt[: R // 2]
-    ys[me, :, own:2 * own] = yt[R // 2:]
+    h = n // 2
+    top = samples // 2
+    base = me // h * h
+    targets = [base + lax.rem(me + k, h) for k in range(h)] + [h - base + lax.rem(me + k, h) for k in range(h)]
 
     barrier = pltpu.get_barrier_semaphore()
     for k in range(1, n):
-        pl.semaphore_signal(barrier, inc=1, device_id={"smp": lax.rem(me + k, n)})
-    pl.semaphore_wait(barrier, n - 1)
-
-    coal_copies, y_copies = [], []
-    for k in range(1, n):
-        copy = pltpu.make_async_remote_copy(
-            src_ref=coal.at[me], dst_ref=coal.at[me], send_sem=send_c.at[k], recv_sem=recv_c.at[k],
-            device_id={"smp": lax.rem(me + k, n)})
-        copy.start()
-        coal_copies.append(copy)
-    for k in range(1, n):
-        copy = pltpu.make_async_remote_copy(
-            src_ref=ys.at[me], dst_ref=ys.at[me], send_sem=send_y.at[k], recv_sem=recv_y.at[k],
-            device_id={"smp": lax.rem(me + k, n)})
-        copy.start()
-        y_copies.append(copy)
+        pl.semaphore_signal(barrier, inc=1, device_id={"smp": targets[k]})
+
+    loads = [pltpu.make_async_copy(ref, ints.at[i], in_sem.at[i])
+             for i, ref in enumerate((size_in, step_in, shift_in))]
+    loads.append(pltpu.make_async_copy(y_in, y_own, in_sem.at[3]))
+    for load in loads:
+        load.start()
+    for load in loads:
+        load.wait()
+    for i in range(3):
+        coal[0, i:i + 1, 0:own] = ints[i].astype(jnp.float32)
+    yt = y_own[...]
+    ys[0, :, 0:own] = yt[: R // 2]
+    ys[0, :, own:2 * own] = yt[R // 2:]
 
     lane = lax.broadcasted_iota(jnp.int32, (own, LANES), 1)
     one = jnp.full((own, LANES), 1.0, jnp.float32)
-    for k in range(n):
-        peer = lax.rem(me + n - k, n)
-        if k:
-            coal_copies[k - 1].wait_recv()
-        cols = coal[peer].T[0:own].astype(jnp.int32)
+
+    def build(k):
+        cols = coal[k].T[0:own].astype(jnp.int32)
         size = jnp.broadcast_to(cols[:, 0:1], (own, LANES))
         mult = 2 * jnp.broadcast_to(cols[:, 1:2], (own, LANES)) + 1
         shift = jnp.broadcast_to(cols[:, 2:3], (own, LANES))
         code = ((lane * mult + shift) << 20) + LOW
         limit = (size << 20) + LOW
         stride = mult << 27
-        rows = pl.ds(pl.multiple_of(peer * own, own), own)
         for c in range(F // LANES):
-            masks[rows, c * LANES:(c + 1) * LANES] = jnp.where(code < limit, one, -one).astype(masks.dtype)
+            masks[k * own:(k + 1) * own, c * LANES:(c + 1) * LANES] = (
+                jnp.where(code < limit, one, -one).astype(masks.dtype))
             code = code + stride
 
-    m = masks[...]
-    gram = lax.dot_general(m, m, (((1,), (1,)), ((), ())), preferred_element_type=jnp.float32)
-    gram_hi = gram.astype(jnp.bfloat16)
-    gram_lo = (gram - gram_hi.astype(jnp.float32)).astype(jnp.bfloat16)
+    build(0)
+    pl.semaphore_wait(barrier, n - 1)
+
+    def send(buffer, k, rows, send_sem, recv_sem):
+        copy = pltpu.make_async_remote_copy(
+            src_ref=buffer.at[0, pl.ds(0, rows)], dst_ref=buffer.at[k, pl.ds(0, rows)],
+            send_sem=send_sem.at[k], recv_sem=recv_sem.at[k], device_id={"smp": targets[k]})
+        copy.start()
+        return copy
+
+    order = list(range(h, n)) + list(range(1, h))
+    coal_copies = {k: send(coal, k, CODES, send_c, recv_c) for k in order}
+    y_copies = {k: send(ys, k, R // 2, send_y, recv_y) for k in order}
+
+    def halves(v):
+        hi = v.astype(jnp.bfloat16)
+        return hi, (v - hi.astype(jnp.float32)).astype(jnp.bfloat16)
+
+    for k in range(1, h):
+        coal_copies[k].wait_recv()
+        build(k)
+    near = masks[0:top]
+    g00 = halves(mm_nt(near, near))
+    for k in range(h, n):
+        coal_copies[k].wait_recv()
+        build(k)
+    far = masks[top:samples]
+    g01 = halves(mm_nt(masks[0:top], far))
+    g11 = halves(mm_nt(far, far))
 
     def by_gram(v):
         s = split(v)
-        return join(mm(s, gram_hi) + mm(s, gram_lo), R)
+        s0, s1 = s[:, :top], s[:, top:]
+        first = (mm(s0, g00[0]) + mm_nt(s1, g01[0])) + (mm(s0, g00[1]) + mm_nt(s1, g01[1]))
+        second = (mm(s0, g01[0]) + mm(s1, g11[0])) + (mm(s0, g01[1]) + mm(s1, g11[1]))
+        return join(jnp.concatenate([first, second], axis=1), R)
 
     left = lax.broadcasted_iota(jnp.int32, (R // 2, LANES), 1) < own
     kf, y = [], []
-    for copy in y_copies:
-        copy.wait_recv()
+    for k in order:
+        y_copies[k].wait_recv()
     for q in range(0, n, 2):
         t0, t1 = coal[q, 0:1], coal[q + 1, 0:1]
         kf.append(jnp.where(left[0:1], t0, pltpu.roll(t1, own, 1)))
@@ -179,11 +207,12 @@
             norm_now = norm_next
 
     place = me * n_feat + lax.axis_index("feat")
-    mine = masks[:, pl.ds(pl.multiple_of(place * share, share), share)]
+    mine = masks[:, pl.ds(pl.multiple_of(place * share, share), share)].astype(jnp.bfloat16)
     both = jnp.concatenate([attributions, residual], axis=0)
     out_ref[...] = join(mm(split(both), mine), 2 * R)
-    for copy in coal_copies + y_copies:
-        copy.wait_send()
+    for k in order:
+        coal_copies[k].wait_send()
+        y_copies[k].wait_send()
 
 
 def gram_body(n, n_feat, coal_size, coal_step, coal_shift, outputs_y):
@@ -192,19 +221,23 @@
     out = pl.pallas_call(
         functools.partial(kernel, n, n_feat),
         out_shape=jax.ShapeDtypeStruct((2 * R, share), jnp.float32),
-        in_specs=[pl.BlockSpec(memory_space=pltpu.VMEM)] * 4,
+        in_specs=[pl.BlockSpec(memory_space=pltpu.HBM)] * 4,
         out_specs=pl.BlockSpec(memory_space=pltpu.VMEM),
         scratch_shapes=[
+            pltpu.VMEM((3, 1, own), jnp.int32),
+            pltpu.VMEM((R, own), jnp.float32),
             pltpu.VMEM((n, 8, LANES), jnp.float32),
             pltpu.VMEM((n, R // 2, LANES), jnp.float32),
-            pltpu.VMEM((own * n, F), jnp.bfloat16),
+            pltpu.VMEM((own * n, F), MASK_TYPE),
+            pltpu.SemaphoreType.DMA((4,)),
             pltpu.SemaphoreType.DMA((n,)),
             pltpu.SemaphoreType.DMA((n,)),
             pltpu.SemaphoreType.DMA((n,)),
             pltpu.SemaphoreType.DMA((n,)),
         ],
-        compiler_params=pltpu.CompilerParams(collective_id=0, has_side_effects=True),
-    )(coal_size.reshape(1, own), coal_step.reshape(1, own), coal_shift.reshape(1, own), outputs_y)
+        compiler_params=pltpu.CompilerParams(
+            collective_id=0, has_side_effects=True, vmem_limit_bytes=VMEM_BYTES),
+    )(coal_size.reshape(1, own), coal_step.reshape(1, own), coal_shift.reshape(1, own), outputs_y.T)
     return out[:R].T, out[R:].T
 
 

time: 19.3 us -> 16 us (0.83)
  Pallas kernels: 15.6 us -> 13.1 us
  local copies, waits for them, and re-layouts: 2.82 us -> 2.01 us
    pallas_call x1, Pallas kernels: 15.6 us -> 13.1 us  [gram_body(): pl.pallas_call(functools.partial(kernel, n, n_feat), out_shape=jax.ShapeD...]
    transpose x1, local copies, waits for them, and re-layouts: 1.4 us -> 0.63 us  [gram_body(): return (out[:R].T, out[R:].T)]
    unnamed x1 -> x8, local copies, waits for them, and re-layouts: 1.41 us -> 1.38 us
where the time goes in v2:
time: 16 us; the launch traced here: 15.7 us
  Pallas kernels  13.1 us (82%)
  local copies, waits for them, and re-layouts  2.01 us (13%)
  between operations  0.66 us (4%)
    pallas_call x1, Pallas kernels, gram_body(): pl.pallas_call(functools.partial(kernel, n, n_feat), out_shape=jax.ShapeD...  13.1 us
    unnamed x8, local copies, waits for them, and re-layouts  1.38 us
    transpose x1, local copies, waits for them, and re-layouts, gram_body(): return (out[:R].T, out[R:].T)  0.63 us

profile of v2, /device:TPU:0, one launch (start us, length us, event | category | flops | bytes accessed | tf_op | source)
XLA Modules:
  0.0 15.7 jit_solution(10640939449645547447)
XLA Ops:
  0.6 0.0 copy-start.1
  0.6 0.0 copy-start.2
  0.7 0.0 copy-start.3
  0.7 0.6 %copy-done.1 = s32[64]{0:T(128)S(1)} copy-done((s32[64]{0:T(128)S(1)}, s32[64]{0:T(128)}, u32[]{:S(2)}) %copy-start.1) | copy-done | bytes 280
  1.3 0.0 copy-done.2
  1.3 0.0 copy-done.3
  1.3 0.0 copy-start
  1.3 0.7 %copy-done = f32[64,32]{0,1:T(8,128)S(1)} copy-done((f32[64,32]{0,1:T(8,128)S(1)}, f32[64,32]{0,1:T(8,128)}, u32[]{:S(2)}) %copy-start) | copy-done | bytes 8216
  2.0 13.1 %shard_map.59 = f32[64,256]{1,0:T(8,128)S(1)} custom-call(s32[1,64]{1,0:T(1,128)S(1)} %bitcast.9, s32[1,64]{1,0:T(1,128)S(1)} %bitcast.10, s32[1,64]{1,0:T(1,128)S(1)} %bitcast.11, f32[32,64]{1,0:T(8,128)S(1)} %bitcast.8), custom_call_target="tpu_custom_call" | custom-call | tf_op jit(solution)/shard_map/pallas_call | solution.py:221
  15.1 0.6 %slice_bitcast_fusion = (f32[256,32]{0,1:T(8,128)}, f32[256,32]{0,1:T(8,128)}) fusion(f32[64,256]{1,0:T(8,128)S(1)} %shard_map.59), kind=kLoop, calls=%fused_computation | loop fusion | bytes 131072 | tf_op jit(solution)/shard_map/transpose | solution.py:241
Async XLA Ops:
  0.6 0.7 %copy-start.1 = (s32[64]{0:T(128)S(1)}, s32[64]{0:T(128)}, u32[]{:S(2)}) copy-start(s32[64]{0:T(128)} %param.4) | copy-start | bytes 772
  0.6 0.7 %copy-start.2 = (s32[64]{0:T(128)S(1)}, s32[64]{0:T(128)}, u32[]{:S(2)}) copy-start(s32[64]{0:T(128)} %param.5) | copy-start | bytes 772
  0.7 0.7 %copy-start.3 = (s32[64]{0:T(128)S(1)}, s32[64]{0:T(128)}, u32[]{:S(2)}) copy-start(s32[64]{0:T(128)} %param.6) | copy-start | bytes 772
  1.3 0.7 %copy-start = (f32[64,32]{0,1:T(8,128)S(1)}, f32[64,32]{0,1:T(8,128)}, u32[]{:S(2)}) copy-start(f32[64,32]{0,1:T(8,128)} %param.7) | copy-start | bytes 24580
